TPU v7x, 256 devices: a whole 4x4x8 slice. The times are simulated.
256 devices in a mesh: node: 64 (over y, z, core), feat: 4 (over x).
Axes of the slice: x: 4, y: 4, z: 8, core: 2. Of those that a mesh axis runs over, the one named last changes fastest.
Arguments:
- features: bfloat16 [32768, 128], P('node', 'feat'), may hold values from -10 to 10
- send_rows: int32 [64, 64, 64], P('node'), may hold values from 0 to 511
- send_count: int32 [64, 64], P('node'), may hold values from 1 to 64, 2048 in all within a row
- tile_src: int32 [256, 16], P('node'), may hold values from 0 to 35
- tile_val: bfloat16 [256, 16, 128, 128], P('node'), may hold values from 0 to 0.0009765625
- labels: int32 [32768], P('node'), may hold values from 0 to 171
- w_self1: bfloat16 [128, 1024], P('feat'), may hold values from -0.5 to 0.5
- w_neigh1: bfloat16 [128, 1024], P('feat'), may hold values from -0.5 to 0.5
- w_self2: bfloat16 [1024, 172], P('feat'), may hold values from -0.5 to 0.5
- w_neigh2: bfloat16 [1024, 172], P('feat'), may hold values from -0.1875 to 0.1875
Outputs:
- mean_loss: float32 [], replicated
- grad_self1: float32 [128, 1024], P('feat')
- grad_neigh1: float32 [128, 1024], P('feat')
- grad_self2: float32 [1024, 172], P('feat')
- grad_neigh2: float32 [1024, 172], P('feat')
Inputs may be any that keep to these rules, and one draw needn't show every extreme that they name: `send_rows`: row indices within the sending partition's 512 rows. Each row of send_count sums to 2048 and holds 64 at least once. `tile_src`: block numbers of the destination partition's source rows: numbers below 4 name its own rows, the others its halo slots.
All inputs are finite; a program needn't handle non-finite values.
Results may differ from a plain program's by a relative error of at most 0.00095.
The roundings to bfloat16 on the way count: a program that leaves them out, or rounds other values in their place, can miss the bound.
Values may be sent and summed in bfloat16 or wider, within the bound.
A program may use at most 64 MiB of HBM per device.

v0:
```python
import math
import jax
import jax.numpy as jnp
from jax import lax
from jax.sharding import PartitionSpec as P


def pack_rows(own_rows, send_rows, send_count):
    slot_total = send_rows.shape[2]
    picked = jnp.take(own_rows, send_rows[0].reshape(-1), axis=0)
    picked = picked.reshape(send_rows.shape[1], slot_total, own_rows.shape[1])
    in_use = jnp.arange(slot_total, dtype=jnp.int32)[None, :] < send_count[0][:, None]
    return jnp.where(in_use[:, :, None], picked, jnp.zeros_like(picked))


def aggregate(own_rows, arrived, tile_src, tile_val):
    col_count = own_rows.shape[1]
    blocks = jnp.concatenate([own_rows, arrived], axis=0).reshape(-1, 128, col_count)
    chosen = jnp.take(blocks, tile_src, axis=0)
    summed = jnp.einsum("bkij,bkjh->bih", tile_val, chosen, preferred_element_type=jnp.float32)
    return summed.reshape(own_rows.shape[0], col_count).astype(jnp.bfloat16)


def spread_back(grads, tile_src, tile_val, src_total):
    col_count = grads.shape[1]
    per_tile = jnp.einsum(
        "bkij,bih->bkjh",
        tile_val,
        grads.reshape(-1, 128, col_count),
        preferred_element_type=jnp.float32,
    )
    one_hot = (
        tile_src.reshape(-1)[None, :] == jnp.arange(src_total // 128, dtype=jnp.int32)[:, None]
    ).astype(jnp.float32)
    landed = jnp.dot(
        one_hot,
        per_tile.reshape(one_hot.shape[1], -1),
        precision=lax.Precision.HIGHEST,
        preferred_element_type=jnp.float32,
    )
    return landed.reshape(src_total, col_count)


def cross_entropy(logits, labels, grad_scale):
    row_max = jnp.max(logits, axis=1, keepdims=True)
    shifted = logits - row_max
    total_exp = jnp.sum(jnp.exp(shifted), axis=1, keepdims=True)
    classes = jnp.arange(logits.shape[1], dtype=jnp.int32)
    target = (labels[:, None] == classes[None, :]).astype(jnp.float32)
    row_loss = jnp.log(total_exp)[:, 0] - jnp.sum(shifted * target, axis=1)
    grads = ((jnp.exp(shifted) / total_exp - target) * grad_scale).astype(jnp.bfloat16)
    return (row_loss, grads)


def shards(
    features,
    send_rows,
    send_count,
    tile_src,
    tile_val,
    labels,
    w_self1,
    w_neigh1,
    w_self2,
    w_neigh2,
):
    node_count = lax.axis_size("node")
    own_count = features.shape[0]
    slot_total = send_rows.shape[2]
    src_total = own_count + node_count * slot_total
    node_total = own_count * node_count
    grad_scale = 1.0 / math.sqrt(node_total)
    outgoing = pack_rows(features, send_rows, send_count)
    arrived = lax.all_to_all(outgoing, "node", split_axis=0, concat_axis=0, tiled=True).reshape(
        -1, features.shape[1]
    )
    agg_one = aggregate(features, arrived, tile_src, tile_val)
    partial_one = jnp.dot(features, w_self1, preferred_element_type=jnp.float32)
    partial_one = partial_one + jnp.dot(agg_one, w_neigh1, preferred_element_type=jnp.float32)
    pre_act = lax.psum_scatter(partial_one, "feat", scatter_dimension=1, tiled=True)
    activated, pullback = jax.vjp(lambda inner: jax.nn.gelu(inner, approximate=True), pre_act)
    hidden = activated.astype(jnp.bfloat16)
    unit_count = hidden.shape[1]
    outgoing_two = pack_rows(hidden, send_rows, send_count)
    arrived_two = lax.all_to_all(
        outgoing_two, "node", split_axis=0, concat_axis=0, tiled=True
    ).reshape(-1, unit_count)
    agg_two = aggregate(hidden, arrived_two, tile_src, tile_val)
    partial_two = jnp.dot(hidden, w_self2, preferred_element_type=jnp.float32)
    partial_two = partial_two + jnp.dot(agg_two, w_neigh2, preferred_element_type=jnp.float32)
    logits = lax.psum(partial_two, "feat")
    row_loss, dlogits = cross_entropy(logits, labels, grad_scale)
    mean_loss = lax.psum(jnp.sum(row_loss), "node") / node_total
    grad_pair = lax.psum(
        (
            jnp.einsum("nh,nc->hc", hidden, dlogits, preferred_element_type=jnp.float32),
            jnp.einsum("nh,nc->hc", agg_two, dlogits, preferred_element_type=jnp.float32),
        ),
        "node",
    )
    back_grad = jnp.einsum(
        "nc,hc->nh", dlogits, w_neigh2, preferred_element_type=jnp.float32
    ).astype(jnp.bfloat16)
    direct = jnp.einsum("nc,hc->nh", dlogits, w_self2, preferred_element_type=jnp.float32)
    landed = spread_back(back_grad, tile_src, tile_val, src_total)
    halo_back = landed[own_count:].reshape(node_count, slot_total, unit_count)
    returned = lax.all_to_all(
        halo_back.astype(jnp.bfloat16), "node", split_axis=0, concat_axis=0, tiled=True
    ).astype(halo_back.dtype)
    in_use = jnp.arange(slot_total, dtype=jnp.int32)[None, :] < send_count[0][:, None]
    returned = jnp.where(in_use[:, :, None], returned, jnp.zeros_like(returned))
    back_rows = jax.ops.segment_sum(
        returned.reshape(-1, unit_count), send_rows[0].reshape(-1), num_segments=own_count
    )
    back_hidden = direct + landed[:own_count] + back_rows
    pre_grad = pullback(back_hidden)[0].astype(jnp.bfloat16)
    shard_piece = lax.all_gather(pre_grad, "feat", axis=1, tiled=True)
    local_grads = jnp.stack(
        [
            jnp.einsum("nf,nh->fh", features, shard_piece, preferred_element_type=jnp.float32),
            jnp.einsum("nf,nh->fh", agg_one, shard_piece, preferred_element_type=jnp.float32),
        ]
    )
    summed = lax.psum(local_grads, "node")
    return (mean_loss, summed[0], summed[1], grad_pair[0], grad_pair[1])


def solution(mesh):
    in_specs = (
        P("node", "feat"),
        P("node", None, None),
        P("node", None),
        P("node", None),
        P("node", None, None, None),
        P("node"),
        P("feat", None),
        P("feat", None),
        P("feat", None),
        P("feat", None),
    )
    out_specs = (P(), P("feat", None), P("feat", None), P("feat", None), P("feat", None))
    return jax.shard_map(shards, mesh=mesh, in_specs=in_specs, out_specs=out_specs, check_vma=False)
```

profile of v0, /device:TPU:2, one launch (start us, length us, event | category | flops | bytes accessed | tf_op | source)
XLA Modules:
  0.0 571.0 jit_solution(3139560621322994043)
XLA Ops:
  7.2 1.0 reshape_squeeze.7
  8.2 0.9 iota_compare_fusion.1
  9.1 0.9 copy.35
  10.0 12.1 %gather_fusion = bf16[4096,32]{1,0:T(8,128)(2,1)S(1)} fusion(bf16[512,32]{1,0:T(8,128)(2,1)S(1)} %copy.35, s32[4096]{0:T(1024)S(1)} %broadcast_clamp_fusion), kind=kCustom, calls=%fused_computation | custom fusion | bytes 540672 | tf_op jit(solution)/shard_map/jit(_take)/gather | solution.py:10
  22.1 1.1 copy.36
  23.3 1.2 fusion.30
  24.4 1.0 reshape.178
  25.4 12.1 %all-to-all-start = ((bf16[64,2,1024]{2,1,0:T(2,128)(2,1)}), bf16[64,2,1024]{2,1,0:T(2,128)(2,1)S(1)}, u32[]{:S(2)}, u32[]{:S(2)}) async-start(bf16[64,2,1024]{2,1,0:T(2,128)(2,1)} %reshape.178), calls=%async_computation | async-start | bytes 524288 | tf_op jit(solution)/shard_map/all_to_all | solution.py:74
  37.5 0.0 reduce-scatter.2.cloned.1.call-start
  37.6 0.1 reshape.140
  37.7 1.8 fusion.31
  39.5 10.0 %all-to-all-done = bf16[64,2,1024]{2,1,0:T(2,128)(2,1)S(1)} async-done(((bf16[64,2,1024]{2,1,0:T(2,128)(2,1)}), bf16[64,2,1024]{2,1,0:T(2,128)(2,1)S(1)}, u32[]{:S(2)}, u32[]{:S(2)}) %all-to-all-start) | async-done | bytes 262176 | tf_op jit(solution)/shard_map/all_to_all | solution.py:74
  49.5 0.3 reshape.179
  49.9 0.2 copy.37
  50.1 0.5 reshape.123
  50.6 0.1 copy_bitcast_fusion
  50.6 0.7 gather_fusion.1
  51.3 0.8 fusion.11
  52.1 0.7 copy-done.3
  52.9 1.8 convolution_add_fusion
  54.7 28.0 %reduce-scatter.2.cloned.1.call-done = f32[512,256]{1,0:T(8,128)} async-done(((f32[512,1024]{1,0:T(8,128)}), f32[512,256]{1,0:T(8,128)}) %reduce-scatter.2.cloned.1.call-update) | async-done | bytes 524304 | tf_op jit(solution)/shard_map/reduce_scatter | solution.py:80
  82.7 1.2 multiply_convert_fusion
  83.9 16.9 %gather_fusion.2 = bf16[4096,256]{1,0:T(8,128)(2,1)} fusion(bf16[512,256]{1,0:T(8,128)(2,1)S(1)} %multiply_convert_fusion, s32[4096]{0:T(1024)S(1)} %broadcast_clamp_fusion), kind=kCustom, calls=%fused_computation.2 | custom fusion | bytes 4210688 | tf_op jit(solution)/shard_map/jit(_take)/gather | solution.py:10
  100.8 4.4 select_select_fusion
  105.2 10.9 %all-to-all-start.1 = ((bf16[64,64,256]{2,1,0:T(8,128)(2,1)}), bf16[64,64,256]{2,1,0:T(8,128)(2,1)}, u32[]{:S(2)}, u32[]{:S(2)}) async-start(bf16[64,64,256]{2,1,0:T(8,128)(2,1)} %select_select_fusion), calls=%async_computation.2 | async-start | bytes 4194304 | tf_op jit(solution)/shard_map/all_to_all | solution.py:85
  116.1 0.2 fusion.32
  116.4 50.7 %all-to-all-done.1 = bf16[64,64,256]{2,1,0:T(8,128)(2,1)} async-done(((bf16[64,64,256]{2,1,0:T(8,128)(2,1)}), bf16[64,64,256]{2,1,0:T(8,128)(2,1)}, u32[]{:S(2)}, u32[]{:S(2)}) %all-to-all-start.1) | async-done | bytes 2097184 | tf_op jit(solution)/shard_map/all_to_all | solution.py:85
  167.1 3.2 pad_maximum_fusion
  170.3 4.4 gather_fusion.3
  174.7 3.2 fusion.7
  178.0 1.0 convolution_add_fusion.2
  179.0 0.1 eq.31
  179.0 42.6 %all-reduce.4.cloned.1.call-done = f32[512,172]{0,1:T(8,128)} async-done(((f32[512,172]{0,1:T(8,128)}), f32[512,172]{0,1:T(8,128)}) %all-reduce.4.cloned.1.call-update) | async-done | bytes 352272 | tf_op jit(solution)/shard_map/psum | solution.py:91
  221.7 1.0 reduce_max.9
  222.7 1.1 exponential_reduce_fusion
  223.8 1.1 multiply_convert_fusion.1
  224.9 0.3 convolution_convert_fusion
  225.2 4.5 convolution_bitcast_fusion
  229.7 8.7 %copy.41 = f32[4,16,128,256]{3,2,1,0:T(8,128)} copy(f32[4,16,128,256]{2,3,1,0:T(8,128)} %convolution_bitcast_fusion) | data formatting | bytes 16777216 | tf_op jit(solution)/shard_map/bkij,bih->bkjh/dot_general | solution.py:26
  238.4 8.1 %copy.49 = f32[8,8,128,256]{3,1,2,0:T(8,128)S(1)} copy(f32[8,8,128,256]{3,2,1,0:T(8,128)} %bitcast.90) | data formatting | bytes 16777216
  246.5 4.3 fusion.26
  250.8 2.3 copy-done.2
  253.1 0.3 slice.37
  253.4 2.4 convert_element_type.51
  255.9 10.9 %all-to-all-start.2 = ((bf16[64,64,256]{2,1,0:T(8,128)(2,1)}), bf16[64,64,256]{2,1,0:T(8,128)(2,1)}, u32[]{:S(2)}, u32[]{:S(2)}) async-start(bf16[64,64,256]{2,1,0:T(8,128)(2,1)} %convert_element_type.51), calls=%async_computation.3 | async-start | bytes 4194304 | tf_op jit(solution)/shard_map/all_to_all | solution.py:107
  266.8 0.1 reshape.164
  266.9 0.4 slice.18
  267.2 0.3 convolution_add_fusion.1
  267.5 50.3 %all-to-all-done.2 = bf16[64,64,256]{2,1,0:T(8,128)(2,1)} async-done(((bf16[64,64,256]{2,1,0:T(8,128)(2,1)}), bf16[64,64,256]{2,1,0:T(8,128)(2,1)}, u32[]{:S(2)}, u32[]{:S(2)}) %all-to-all-start.2) | async-done | bytes 2097184 | tf_op jit(solution)/shard_map/all_to_all | solution.py:107
  317.8 3.5 convert_select_fusion
  321.3 23.3 %scatter_fusion = f32[512,256]{1,0:T(8,128)S(1)} fusion(f32[512,256]{1,0:T(8,128)S(1)} %convolution_add_fusion.1, s32[4096]{0:T(1024)S(1)} %reshape.164, f32[4096,256]{1,0:T(8,128)} %bitcast.92), kind=kCustom, calls=%fused_computation.4 | custom fusion | flops 1048576 | bytes 12599296 | tf_op jit(solution)/shard_map/scatter-add | solution.py:112
  344.6 1.1 fusion.18
  345.7 0.9 fusion.34
  346.6 0.9 fusion.33
  347.5 23.0 %all-gather.2.cloned.1.call-done = bf16[512,1024]{1,0:T(8,128)(2,1)} async-done(((bf16[512,256]{1,0:T(8,128)(2,1)}), bf16[512,1024]{1,0:T(8,128)(2,1)}) %all-gather.2.cloned.1.call-update) | async-done | bytes 1048592 | tf_op jit(solution)/shard_map/all_gather | solution.py:117
  370.5 1.7 convolution_bitcast_fusion.2
  372.2 1.5 convolution_bitcast_fusion.1
  373.7 0.7 pad_maximum_fusion.1
  374.4 0.6 subtract_reduce_fusion
  375.0 128.7 %psum.36 = f32[]{:T(128)} all-reduce(f32[]{:T(128)} %subtract_reduce_fusion), channel_id=1, replica_groups=mesh['node'=64,'feat'=4] {'node'}, use_global_device_ids=true, to_apply=%region_6.7 | all-reduce | flops 1 | bytes 8 | tf_op jit(solution)/shard_map/psum | solution.py:93
  504.4 54.0 %all-reduce.6.cloned.1.call-done = (f32[2,32,1024]{2,1,0:T(8,128)}, f32[256,172]{0,1:T(8,128)}, f32[256,172]{0,1:T(8,128)}) async-done(((f32[2,32,1024]{2,1,0:T(8,128)}, f32[256,172]{0,1:T(8,128)}, f32[256,172]{0,1:T(8,128)}), (f32[2,32,1024]{2,1,0:T(8,128)}, f32[256,172]{0,1:T(8,128)}, f32[256,172]{0,1:T(8,128)})) %all-reduce.6.cloned.1.call-update) | async-done | bytes 614416 | tf_op jit(solution)/shard_map/psum | solution.py:124
  558.4 1.7 slice_bitcast_fusion
  560.1 1.6 copy.64
  561.7 1.6 copy.65
  (38 shorter events, 0.3 us)
Async XLA Ops:
  7.2 44.1 %copy-start = (bf16[4,16,128,128]{3,2,1,0:T(8,128)(2,1)S(1)}, bf16[4,16,128,128]{3,2,1,0:T(8,128)(2,1)}, u32[]{:S(2)}) copy-start(bf16[4,16,128,128]{3,2,1,0:T(8,128)(2,1)} %param.14) | copy-start | bytes 6291460
  22.1 15.5 %copy-start.11 = (s32[4,16]{1,0:T(4,128)S(1)}, s32[4,16]{1,0:T(4,128)}, u32[]{:S(2)}) copy-start(s32[4,16]{1,0:T(4,128)} %param.13) | copy-start | bytes 772
  22.1 15.6 %copy-start.5 = (bf16[512,32]{0,1:T(8,128)(2,1)S(1)}, bf16[512,32]{0,1:T(8,128)(2,1)}, u32[]{:S(2)}) copy-start(bf16[512,32]{0,1:T(8,128)(2,1)} %param.10) | copy-start | bytes 98308
  22.1 15.6 %copy-start.10 = (bf16[32,1024]{1,0:T(8,128)(2,1)S(1)}, bf16[32,1024]{1,0:T(8,128)(2,1)}, u32[]{:S(2)}) copy-start(bf16[32,1024]{1,0:T(8,128)(2,1)} %param.16) | copy-start | bytes 196612
  25.4 24.1 %all-to-all-start = ((bf16[64,2,1024]{2,1,0:T(2,128)(2,1)}), bf16[64,2,1024]{2,1,0:T(2,128)(2,1)S(1)}, u32[]{:S(2)}, u32[]{:S(2)}) async-start(bf16[64,2,1024]{2,1,0:T(2,128)(2,1)} %reshape.178), calls=%async_computation | async-start | bytes 524288 | tf_op jit(solution)/shard_map/all_to_all | solution.py:74
  37.5 45.1 %reduce-scatter.2.cloned.1.call-start = ((), (), s32[]{:S(2)}) async-start(), calls=%async_computation.4 | async-start | bytes 2621440 | tf_op jit(solution)/shard_map/reduce_scatter | solution.py:80
  51.3 1.6 copy-start.3
  51.3 1.6 copy-start.9
  105.2 10.9 %copy-start.7 = (bf16[256,172]{0,1:T(8,128)(2,1)S(1)}, bf16[256,172]{0,1:T(8,128)(2,1)}, u32[]{:S(2)}) copy-start(bf16[256,172]{0,1:T(8,128)(2,1)} %param.18) | copy-start | bytes 264196
  105.2 61.9 %all-to-all-start.1 = ((bf16[64,64,256]{2,1,0:T(8,128)(2,1)}), bf16[64,64,256]{2,1,0:T(8,128)(2,1)}, u32[]{:S(2)}, u32[]{:S(2)}) async-start(bf16[64,64,256]{2,1,0:T(8,128)(2,1)} %select_select_fusion), calls=%async_computation.2 | async-start | bytes 4194304 | tf_op jit(solution)/shard_map/all_to_all | solution.py:85
  116.1 105.6 %all-reduce.4.cloned.1.call-start = ((), (), s32[]{:S(2)}) async-start(), calls=%async_computation.5 | async-start | bytes 720896 | tf_op jit(solution)/shard_map/psum | solution.py:91
  174.7 3.2 copy-start.6
  174.7 48.0 %copy-start.12 = (s32[512]{0:T(512)S(1)}, s32[512]{0:T(512)}, u32[]{:S(2)}) copy-start(s32[512]{0:T(512)} %param.15) | copy-start | bytes 6148
  250.8 2.3 copy-start.2
  255.9 10.9 %copy-start.8 = (s32[1,64,64]{2,1,0:T(8,128)S(1)}, s32[1,64,64]{2,1,0:T(8,128)}, u32[]{:S(2)}) copy-start(s32[1,64,64]{2,1,0:T(8,128)} %param.11) | copy-start | bytes 49156
  255.9 11.0 %slice-start = ((f32[36,32768]{1,0:T(8,128)}), f32[4,32768]{1,0:T(4,128)S(1)}, s32[]{:S(2)}) async-start(f32[36,32768]{1,0:T(8,128)} %copy-done.2), calls=%async_computation.8 | async-start | bytes 1048576 | tf_op jit(solution)/shard_map/slice | solution.py:115
  255.9 61.9 %all-to-all-start.2 = ((bf16[64,64,256]{2,1,0:T(8,128)(2,1)}), bf16[64,64,256]{2,1,0:T(8,128)(2,1)}, u32[]{:S(2)}, u32[]{:S(2)}) async-start(bf16[64,64,256]{2,1,0:T(8,128)(2,1)} %convert_element_type.51), calls=%async_computation.3 | async-start | bytes 4194304 | tf_op jit(solution)/shard_map/all_to_all | solution.py:107
  266.7 103.8 %all-gather.2.cloned.1.call-start = ((), (), s32[]{:S(2)}) async-start(), calls=%async_computation.6 | async-start | bytes 1310720 | tf_op jit(solution)/shard_map/all_gather | solution.py:117
  321.3 23.3 %copy-start.4 = (f32[512,256]{1,0:T(8,128)S(1)}, f32[512,256]{1,0:T(8,128)}, u32[]{:S(2)}) copy-start(f32[512,256]{1,0:T(8,128)} %reduce-scatter.2.cloned.1.call-done) | copy-start | bytes 1572868
  345.7 212.8 %all-reduce.6.cloned.1.call-start = ((), (), s32[]{:S(2)}) async-start(), calls=%async_computation.7 | async-start | bytes 1245184 | tf_op jit(solution)/shard_map/psum | solution.py:124
  370.5 192.8 %copy-start.1 = (bf16[4,16,128,128]{3,2,1,0:T(8,128)(2,1)S(1)}, bf16[4,16,128,128]{3,2,1,0:T(8,128)(2,1)}, u32[]{:S(2)}) copy-start(bf16[4,16,128,128]{3,2,1,0:T(8,128)(2,1)} %param.14) | copy-start | bytes 6291460
Sparse Core Ops, SparseCore 0:
  54.8 27.8 reduce-scatter.1
  179.1 42.5 all-reduce.3
  345.8 24.6 all-gather.1
  375.2 183.2 all-reduce.5
where the time goes:
time: 572 us; the launch traced here: 571 us
  waiting for transfers between devices  259 us (45%)
  blocking collectives  129 us (23%)
  local copies, waits for them, and re-layouts  67.3 us (12%)
  other arithmetic  43.3 us (8%)
  starting transfers between devices  34 us (6%)
  matrix products  23.1 us (4%)
  between operations  15.8 us (3%)
    psum x1, blocking collectives, shards(): mean_loss = lax.psum(jnp.sum(row_loss), 'node') / node_total  129 us
    psum x1, waiting for transfers between devices, shards(): summed = lax.psum(local_grads, 'node')  54 us
    all_to_all x1, waiting for transfers between devices, shards(): lax.all_to_all(outgoing_two, 'node', split_axis=0, concat_axis=0, tiled=T...  50.7 us
    all_to_all x1, waiting for transfers between devices, shards(): lax.all_to_all(halo_back.astype(jnp.bfloat16), 'node', split_axis=0, conc...  50.3 us
    psum x1, waiting for transfers between devices, shards(): logits = lax.psum(partial_two, 'feat')  42.6 us
    gather x3, local copies, waits for them, and re-layouts, pack_rows(): picked = jnp.take(own_rows, send_rows[0].reshape(-1), axis=0)  30.2 us
    reduce_scatter x1, waiting for transfers between devices, shards(): lax.psum_scatter(partial_one, 'feat', scatter_dimension=1, tiled=True)  28 us
    scatter-add x1, other arithmetic, shards(): jax.ops.segment_sum(returned.reshape(-1, unit_count), send_rows[0].reshap...  23.3 us
  transfers between devices with their start and end apart: 7, of which 7 were waited for; matrix products, arithmetic and copies ran while one was open for 1% of the time, Pallas kernels for 0%

commit v1 on v0

--- a/solution.py
+++ b/solution.py
@@ -114,7 +114,11 @@
     )
     back_hidden = direct + landed[:own_count] + back_rows
     pre_grad = pullback(back_hidden)[0].astype(jnp.bfloat16)
-    shard_piece = lax.all_gather(pre_grad, "feat", axis=1, tiled=True)
+    block_next = lax.axis_size("feat")
+    mixed_arr = jnp.concatenate([pre_grad] * block_next, 1)
+    shard_piece = lax.all_to_all(
+        mixed_arr, axis_name="feat", split_axis=1, concat_axis=1, tiled=True
+    )
     local_grads = jnp.stack(
         [
             jnp.einsum("nf,nh->fh", features, shard_piece, preferred_element_type=jnp.float32),

time: 572 us -> 559 us (0.977)
  waiting for transfers between devices: 259 us -> 245 us
    all_gather x1 -> x0, waiting for transfers between devices: 23 us -> none  [shards(): shard_piece = lax.all_gather(pre_grad, 'feat', axis=1, tiled=True)]
    all_to_all x0 -> x1, waiting for transfers between devices: none -> 12.4 us  [shards(): lax.all_to_all(mixed_arr, axis_name='feat', split_axis=1, concat_axis=1,...]
where the time goes in v1:
time: 559 us; the launch traced here: 557 us
  waiting for transfers between devices  245 us (44%)
  blocking collectives  125 us (22%)
  local copies, waits for them, and re-layouts  69 us (12%)
  other arithmetic  42.7 us (8%)
  starting transfers between devices  38.9 us (7%)
  matrix products  20.7 us (4%)
  between operations  15.9 us (3%)
    psum x1, blocking collectives, shards(): mean_loss = lax.psum(jnp.sum(row_loss), 'node') / node_total  125 us
    psum x1, waiting for transfers between devices, shards(): summed = lax.psum(local_grads, 'node')  51.2 us
    all_to_all x1, waiting for transfers between devices, shards(): lax.all_to_all(outgoing_two, 'node', split_axis=0, concat_axis=0, tiled=T...  50.7 us
    all_to_all x1, waiting for transfers between devices, shards(): lax.all_to_all(halo_back.astype(jnp.bfloat16), 'node', split_axis=0, conc...  50.3 us
    psum x1, waiting for transfers between devices, shards(): logits = lax.psum(partial_two, 'feat')  42.6 us
    gather x3, local copies, waits for them, and re-layouts, pack_rows(): picked = jnp.take(own_rows, send_rows[0].reshape(-1), axis=0)  30.3 us
    reduce_scatter x1, waiting for transfers between devices, shards(): lax.psum_scatter(partial_one, 'feat', scatter_dimension=1, tiled=True)  28 us
    scatter-add x1, other arithmetic, shards(): jax.ops.segment_sum(returned.reshape(-1, unit_count), send_rows[0].reshap...  23.3 us
  transfers between devices with their start and end apart: 7, of which 7 were waited for; matrix products, arithmetic and copies ran while one was open for 1% of the time, Pallas kernels for 0%

profile of v1, /device:TPU:2, one launch (start us, length us, event | category | flops | bytes accessed | tf_op | source)
XLA Modules:
  0.0 557.4 jit_solution(8991511715885218254)
XLA Ops:
  7.2 1.0 reshape_squeeze.7
  8.2 0.9 iota_compare_fusion.1
  9.1 0.9 copy.36
  10.0 12.1 %gather_fusion = bf16[4096,32]{1,0:T(8,128)(2,1)S(1)} fusion(bf16[512,32]{1,0:T(8,128)(2,1)S(1)} %copy.36, s32[4096]{0:T(1024)S(1)} %broadcast_clamp_fusion), kind=kCustom, calls=%fused_computation | custom fusion | bytes 540672 | tf_op jit(solution)/shard_map/jit(_take)/gather | solution.py:10
  22.1 1.1 copy.37
  23.3 1.2 fusion.30
  24.4 1.0 reshape.181
  25.4 12.1 %all-to-all-start = ((bf16[64,2,1024]{2,1,0:T(2,128)(2,1)}), bf16[64,2,1024]{2,1,0:T(2,128)(2,1)S(1)}, u32[]{:S(2)}, u32[]{:S(2)}) async-start(bf16[64,2,1024]{2,1,0:T(2,128)(2,1)} %reshape.181), calls=%async_computation | async-start | bytes 524288 | tf_op jit(solution)/shard_map/all_to_all | solution.py:74
  37.6 0.1 reshape.143
  37.7 1.8 fusion.31
  39.5 10.0 %all-to-all-done = bf16[64,2,1024]{2,1,0:T(2,128)(2,1)S(1)} async-done(((bf16[64,2,1024]{2,1,0:T(2,128)(2,1)}), bf16[64,2,1024]{2,1,0:T(2,128)(2,1)S(1)}, u32[]{:S(2)}, u32[]{:S(2)}) %all-to-all-start) | async-done | bytes 262176 | tf_op jit(solution)/shard_map/all_to_all | solution.py:74
  49.5 0.3 reshape.182
  49.9 0.2 copy.38
  50.1 0.5 reshape.126
  50.6 0.7 gather_fusion.1
  51.3 0.8 fusion.11
  52.1 0.7 copy-done.3
  52.9 1.8 convolution_add_fusion
  54.7 28.0 %reduce-scatter.2.cloned.1.call-done = f32[512,256]{1,0:T(8,128)} async-done(((f32[512,1024]{1,0:T(8,128)}), f32[512,256]{1,0:T(8,128)}) %reduce-scatter.2.cloned.1.call-update) | async-done | bytes 524304 | tf_op jit(solution)/shard_map/reduce_scatter | solution.py:80
  82.7 1.2 multiply_convert_fusion
  83.9 17.0 %gather_fusion.2 = bf16[4096,256]{1,0:T(8,128)(2,1)} fusion(bf16[512,256]{1,0:T(8,128)(2,1)S(1)} %multiply_convert_fusion, s32[4096]{0:T(1024)S(1)} %broadcast_clamp_fusion), kind=kCustom, calls=%fused_computation.2 | custom fusion | bytes 4210688 | tf_op jit(solution)/shard_map/jit(_take)/gather | solution.py:10
  101.0 4.4 select_select_fusion
  105.3 10.8 %all-to-all-start.1 = ((bf16[64,64,256]{2,1,0:T(8,128)(2,1)}), bf16[64,64,256]{2,1,0:T(8,128)(2,1)}, u32[]{:S(2)}, u32[]{:S(2)}) async-start(bf16[64,64,256]{2,1,0:T(8,128)(2,1)} %select_select_fusion), calls=%async_computation.2 | async-start | bytes 4194304 | tf_op jit(solution)/shard_map/all_to_all | solution.py:85
  116.3 0.2 fusion.32
  116.5 50.7 %all-to-all-done.1 = bf16[64,64,256]{2,1,0:T(8,128)(2,1)} async-done(((bf16[64,64,256]{2,1,0:T(8,128)(2,1)}), bf16[64,64,256]{2,1,0:T(8,128)(2,1)}, u32[]{:S(2)}, u32[]{:S(2)}) %all-to-all-start.1) | async-done | bytes 2097184 | tf_op jit(solution)/shard_map/all_to_all | solution.py:85
  167.2 3.2 pad_maximum_fusion
  170.4 4.4 gather_fusion.3
  174.8 3.2 fusion.7
  178.1 1.0 convolution_add_fusion.2
  179.1 0.1 eq.31
  179.2 42.6 %all-reduce.4.cloned.1.call-done = f32[512,172]{0,1:T(8,128)} async-done(((f32[512,172]{0,1:T(8,128)}), f32[512,172]{0,1:T(8,128)}) %all-reduce.4.cloned.1.call-update) | async-done | bytes 352272 | tf_op jit(solution)/shard_map/psum | solution.py:91
  221.8 1.0 reduce_max.9
  222.8 1.1 exponential_reduce_fusion
  223.9 1.1 multiply_convert_fusion.1
  225.0 0.3 convolution_convert_fusion
  225.3 4.5 convolution_bitcast_fusion
  229.8 8.7 %copy.42 = f32[4,16,128,256]{3,2,1,0:T(8,128)} copy(f32[4,16,128,256]{2,3,1,0:T(8,128)} %convolution_bitcast_fusion) | data formatting | bytes 16777216 | tf_op jit(solution)/shard_map/bkij,bih->bkjh/dot_general | solution.py:26
  238.5 8.1 %copy.53 = f32[8,8,128,256]{3,1,2,0:T(8,128)S(1)} copy(f32[8,8,128,256]{3,2,1,0:T(8,128)} %bitcast.95) | data formatting | bytes 16777216
  246.6 4.3 fusion.26
  250.9 2.3 copy-done.2
  253.2 0.3 slice.37
  253.6 2.5 convert_element_type.53
  256.0 10.9 %all-to-all-start.2 = ((bf16[64,64,256]{2,1,0:T(8,128)(2,1)}), bf16[64,64,256]{2,1,0:T(8,128)(2,1)}, u32[]{:S(2)}, u32[]{:S(2)}) async-start(bf16[64,64,256]{2,1,0:T(8,128)(2,1)} %convert_element_type.53), calls=%async_computation.3 | async-start | bytes 4194304 | tf_op jit(solution)/shard_map/all_to_all | solution.py:107
  267.0 0.4 slice.18
  267.4 0.3 convolution_add_fusion.1
  267.6 50.3 %all-to-all-done.2 = bf16[64,64,256]{2,1,0:T(8,128)(2,1)} async-done(((bf16[64,64,256]{2,1,0:T(8,128)(2,1)}), bf16[64,64,256]{2,1,0:T(8,128)(2,1)}, u32[]{:S(2)}, u32[]{:S(2)}) %all-to-all-start.2) | async-done | bytes 2097184 | tf_op jit(solution)/shard_map/all_to_all | solution.py:107
  317.9 3.5 convert_select_fusion
  321.5 23.3 %scatter_fusion = f32[512,256]{1,0:T(8,128)S(1)} fusion(f32[512,256]{1,0:T(8,128)S(1)} %convolution_add_fusion.1, s32[4096]{0:T(1024)S(1)} %reshape.167, f32[4096,256]{1,0:T(8,128)} %bitcast.97), kind=kCustom, calls=%fused_computation.4 | custom fusion | flops 1048576 | bytes 12599296 | tf_op jit(solution)/shard_map/scatter-add | solution.py:112
  344.8 0.4 fusion.18
  345.2 1.0 copy.64
  346.3 5.0 all-to-all-start.3
  351.3 0.9 fusion.34
  352.2 0.9 fusion.33
  353.1 12.4 %all-to-all-done.3 = bf16[512,4,256]{2,0,1:T(8,128)(2,1)S(1)} async-done(((bf16[512,4,256]{2,0,1:T(8,128)(2,1)}), bf16[512,4,256]{2,0,1:T(8,128)(2,1)S(1)}, u32[]{:S(2)}, u32[]{:S(2)}) %all-to-all-start.3) | async-done | bytes 1048608 | tf_op jit(solution)/shard_map/all_to_all | solution.py:119
  365.5 0.5 copy.44
  366.0 0.4 convolution_bitcast_fusion.1
  366.4 0.4 convolution_bitcast_fusion.2
  366.9 0.7 pad_maximum_fusion.2
  367.6 0.6 subtract_reduce_fusion
  368.2 124.8 %psum.36 = f32[]{:T(128)} all-reduce(f32[]{:T(128)} %subtract_reduce_fusion), channel_id=1, replica_groups=mesh['node'=64,'feat'=4] {'node'}, use_global_device_ids=true, to_apply=%region_6.7 | all-reduce | flops 1 | bytes 8 | tf_op jit(solution)/shard_map/psum | solution.py:93
  493.6 51.2 %all-reduce.6.cloned.1.call-done = (f32[2,32,1024]{2,1,0:T(8,128)}, f32[256,172]{0,1:T(8,128)}, f32[256,172]{0,1:T(8,128)}) async-done(((f32[2,32,1024]{2,1,0:T(8,128)}, f32[256,172]{0,1:T(8,128)}, f32[256,172]{0,1:T(8,128)}), (f32[2,32,1024]{2,1,0:T(8,128)}, f32[256,172]{0,1:T(8,128)}, f32[256,172]{0,1:T(8,128)})) %all-reduce.6.cloned.1.call-update) | async-done | bytes 614416 | tf_op jit(solution)/shard_map/psum | solution.py:128
  544.9 1.7 slice_bitcast_fusion
  546.6 1.6 copy.70
  548.2 1.6 copy.71
  (40 shorter events, 0.4 us)
Async XLA Ops:
  7.2 44.1 %copy-start = (bf16[4,16,128,128]{3,2,1,0:T(8,128)(2,1)S(1)}, bf16[4,16,128,128]{3,2,1,0:T(8,128)(2,1)}, u32[]{:S(2)}) copy-start(bf16[4,16,128,128]{3,2,1,0:T(8,128)(2,1)} %param.14) | copy-start | bytes 6291460
  22.1 15.5 %copy-start.11 = (s32[4,16]{1,0:T(4,128)S(1)}, s32[4,16]{1,0:T(4,128)}, u32[]{:S(2)}) copy-start(s32[4,16]{1,0:T(4,128)} %param.13) | copy-start | bytes 772
  22.1 15.6 %copy-start.5 = (bf16[512,32]{0,1:T(8,128)(2,1)S(1)}, bf16[512,32]{0,1:T(8,128)(2,1)}, u32[]{:S(2)}) copy-start(bf16[512,32]{0,1:T(8,128)(2,1)} %param.10) | copy-start | bytes 98308
  22.1 15.6 %copy-start.10 = (bf16[32,1024]{1,0:T(8,128)(2,1)S(1)}, bf16[32,1024]{1,0:T(8,128)(2,1)}, u32[]{:S(2)}) copy-start(bf16[32,1024]{1,0:T(8,128)(2,1)} %param.16) | copy-start | bytes 196612
  25.4 24.1 %all-to-all-start = ((bf16[64,2,1024]{2,1,0:T(2,128)(2,1)}), bf16[64,2,1024]{2,1,0:T(2,128)(2,1)S(1)}, u32[]{:S(2)}, u32[]{:S(2)}) async-start(bf16[64,2,1024]{2,1,0:T(2,128)(2,1)} %reshape.181), calls=%async_computation | async-start | bytes 524288 | tf_op jit(solution)/shard_map/all_to_all | solution.py:74
  37.6 45.2 %reduce-scatter.2.cloned.1.call-start = ((), (), s32[]{:S(2)}) async-start(), calls=%async_computation.5 | async-start | bytes 2621440 | tf_op jit(solution)/shard_map/reduce_scatter | solution.py:80
  51.3 1.6 copy-start.3
  51.3 1.6 copy-start.9
  105.3 10.9 %copy-start.7 = (bf16[256,172]{0,1:T(8,128)(2,1)S(1)}, bf16[256,172]{0,1:T(8,128)(2,1)}, u32[]{:S(2)}) copy-start(bf16[256,172]{0,1:T(8,128)(2,1)} %param.18) | copy-start | bytes 264196
  105.3 61.9 %all-to-all-start.1 = ((bf16[64,64,256]{2,1,0:T(8,128)(2,1)}), bf16[64,64,256]{2,1,0:T(8,128)(2,1)}, u32[]{:S(2)}, u32[]{:S(2)}) async-start(bf16[64,64,256]{2,1,0:T(8,128)(2,1)} %select_select_fusion), calls=%async_computation.2 | async-start | bytes 4194304 | tf_op jit(solution)/shard_map/all_to_all | solution.py:85
  116.2 105.6 %all-reduce.4.cloned.1.call-start = ((), (), s32[]{:S(2)}) async-start(), calls=%async_computation.6 | async-start | bytes 720896 | tf_op jit(solution)/shard_map/psum | solution.py:91
  174.8 3.2 copy-start.6
  174.8 48.0 %copy-start.12 = (s32[512]{0:T(512)S(1)}, s32[512]{0:T(512)}, u32[]{:S(2)}) copy-start(s32[512]{0:T(512)} %param.15) | copy-start | bytes 6148
  250.9 2.3 copy-start.2
  256.0 10.9 %copy-start.8 = (s32[1,64,64]{2,1,0:T(8,128)S(1)}, s32[1,64,64]{2,1,0:T(8,128)}, u32[]{:S(2)}) copy-start(s32[1,64,64]{2,1,0:T(8,128)} %param.11) | copy-start | bytes 49156
  256.0 11.0 %slice-start = ((f32[36,32768]{1,0:T(8,128)}), f32[4,32768]{1,0:T(4,128)S(1)}, s32[]{:S(2)}) async-start(f32[36,32768]{1,0:T(8,128)} %copy-done.2), calls=%async_computation.8 | async-start | bytes 1048576 | tf_op jit(solution)/shard_map/slice | solution.py:115
  256.0 61.9 %all-to-all-start.2 = ((bf16[64,64,256]{2,1,0:T(8,128)(2,1)}), bf16[64,64,256]{2,1,0:T(8,128)(2,1)}, u32[]{:S(2)}, u32[]{:S(2)}) async-start(bf16[64,64,256]{2,1,0:T(8,128)(2,1)} %convert_element_type.53), calls=%async_computation.3 | async-start | bytes 4194304 | tf_op jit(solution)/shard_map/all_to_all | solution.py:107
  321.5 23.3 %copy-start.4 = (f32[512,256]{1,0:T(8,128)S(1)}, f32[512,256]{1,0:T(8,128)}, u32[]{:S(2)}) copy-start(f32[512,256]{1,0:T(8,128)} %reduce-scatter.2.cloned.1.call-done) | copy-start | bytes 1572868
  346.3 19.2 %all-to-all-start.3 = ((bf16[512,4,256]{2,0,1:T(8,128)(2,1)}), bf16[512,4,256]{2,0,1:T(8,128)(2,1)S(1)}, u32[]{:S(2)}, u32[]{:S(2)}) async-start(bf16[512,4,256]{2,0,1:T(8,128)(2,1)} %bitcast.93), calls=%async_computation.4 | async-start | bytes 2097152 | tf_op jit(solution)/shard_map/all_to_all | solution.py:119
  351.3 193.6 %all-reduce.6.cloned.1.call-start = ((), (), s32[]{:S(2)}) async-start(), calls=%async_computation.7 | async-start | bytes 1245184 | tf_op jit(solution)/shard_map/psum | solution.py:128
  366.0 183.7 %copy-start.1 = (bf16[4,16,128,128]{3,2,1,0:T(8,128)(2,1)S(1)}, bf16[4,16,128,128]{3,2,1,0:T(8,128)(2,1)}, u32[]{:S(2)}) copy-start(bf16[4,16,128,128]{3,2,1,0:T(8,128)(2,1)} %param.14) | copy-start | bytes 6291460
Sparse Core Ops, SparseCore 0:
  54.8 27.8 reduce-scatter.1
  179.2 42.5 all-reduce.3
  367.8 177.0 all-reduce.5
